TPU v7x, 32 devices: a whole 2x2x4 slice. The times are simulated.
32 devices in a mesh: blk: 8 (over z, x), rep: 4 (over y, core).
Axes of the slice: x: 2, y: 2, z: 4, core: 2. Of those that a mesh axis runs over, the one named last changes fastest.
Arguments:
- features: bfloat16 [32768, 128], P('blk'), may hold values from -6 to 6
- weight: bfloat16 [128, 256], replicated, may hold values from -0.5 to 0.5
- bias: float32 [256], replicated, may hold values from -3 to 3
- tile_values: bfloat16 [8, 8, 160, 128, 128], P('blk', 'rep'), may hold values from 0 to 0.041748047
- tile_place: int32 [8, 8, 160], P('blk', 'rep'), may hold values from 0 to 1023, as said below
- tile_count: int32 [8, 8], P('blk', 'rep'), may hold values from 1 to 160, as said below
Outputs:
- activations: bfloat16 [32768, 256], P('blk')
Inputs may be any that keep to these rules, and one draw needn't show every extreme that they name: `tile_place`: within one pair of destination block and section the 160 positions are distinct. `tile_count`: some pair of destination block and section has all 160 slots occupied.
All inputs are finite; a program needn't handle non-finite values.
Results may differ from a plain program's by a relative error of at most 0.0046.
Values may be sent and summed in bfloat16 or wider, within the bound.
A program may use at most 128 MiB of HBM per device.

v0:
```python
import functools

import jax
import jax.numpy as jnp
from jax import lax
from jax.experimental import pallas as pl
from jax.experimental.pallas import tpu as pltpu
from jax.sharding import PartitionSpec as P

MESH = pl.DeviceIdType.MESH
GROUP = 16
BLOCK = 80
CHUNKS = 4
SUBS = 4
ROWS_STEP = 4096
GRANT = 16 * 1024 * 1024


def largest_divisor(number, most):
    return max(d for d in range(1, most + 1) if number % d == 0)


def gather_kernel(blocks, replicas, sections, subs, features_ref, tiles_ref, source_ref, held_ref, ring,
                  ring_send, ring_recv, give_send, give_recv, own_sem, held_sem):
    blk, rep = lax.axis_index("blk"), lax.axis_index("rep")
    share = features_ref.shape[0] // replicas
    sub = share // subs
    odd = lax.rem(blk, 2)
    position = (1 - odd) * lax.div(blk, 2) + odd * (blocks - 1 - lax.div(blk, 2))

    def block_at(offset):
        p = lax.rem(position + blocks + offset, blocks)
        back = lax.div(p, blocks // 2)
        return (1 - back) * (2 * p) + back * (2 * (blocks - 1 - p) + 1)

    def rows(who, h):
        return pl.ds(pl.multiple_of(who * share + h * sub, sub), sub)

    hops = blocks // 2
    ways = (1, -1)
    barrier = pltpu.get_barrier_semaphore()
    for way in ways:
        pl.semaphore_signal(barrier, inc=1, device_id=(block_at(way), rep), device_id_type=MESH)
    for d in range(1, replicas):
        pl.semaphore_signal(barrier, inc=1, device_id=(blk, lax.rem(rep + d, replicas)), device_id_type=MESH)
    pl.semaphore_wait(barrier, replicas + 1)

    def ring_copy(w, k, h):
        source = features_ref.at[rows(rep, h)] if k == 0 else ring.at[w, k - 1, h]
        return pltpu.make_async_remote_copy(
            src_ref=source, dst_ref=ring.at[w, k, h], send_sem=ring_send.at[w, k, h],
            recv_sem=ring_recv.at[w, k, h], device_id=(block_at(ways[w]), rep), device_id_type=MESH)

    def travels(w, k, h):
        return k < hops - 1 or (k == hops - 1 and h * 2 // subs == w)

    for h in range(subs):
        for w in range(2):
            if travels(w, 0, h):
                ring_copy(w, 0, h).start()
    held = pltpu.make_async_copy(tiles_ref, held_ref, held_sem)
    held.start()
    own = pltpu.make_async_copy(features_ref, source_ref.at[0], own_sem)

    @pl.when(rep == 0)
    def _():
        own.start()

    arrivals = [(k, h, w) for k in range(hops) for h in range(subs) for w in range(2) if travels(w, k, h)]

    def give(k, h, w):
        section = lax.rem(blk - block_at(-ways[w] * (k + 1)) + blocks, blocks)
        target, index = lax.div(section, sections), lax.rem(section, sections)
        place = source_ref.at[index, rows(rep, h)]
        here = pltpu.make_async_copy(ring.at[w, k, h], place, give_send.at[w, k, h])
        there = pltpu.make_async_remote_copy(
            src_ref=ring.at[w, k, h], dst_ref=place, send_sem=give_send.at[w, k, h],
            recv_sem=give_recv.at[index, rep, h], device_id=(blk, target), device_id_type=MESH)
        return target, here, there

    for k, h, w in arrivals:
        ring_copy(w, k, h).wait_recv()
        if travels(w, k + 1, h):
            ring_copy(w, k + 1, h).start()
        target, here, there = give(k, h, w)

        @pl.when(target == rep)
        def _():
            here.start()

        @pl.when(target != rep)
        def _():
            there.start()

    for k, h, w in arrivals:
        ring_copy(w, k, h).wait_send()
        target, here, there = give(k, h, w)

        @pl.when(target == rep)
        def _():
            here.wait()

        @pl.when(target != rep)
        def _():
            there.wait_send()

    @pl.when(rep == 0)
    def _():
        own.wait()

    held.wait()
    for index in range(sections):
        def arrive(index=index):
            for d in range(1, replicas):
                giver = lax.rem(rep + d, replicas)
                for h in range(subs):
                    pltpu.make_async_remote_copy(
                        src_ref=ring.at[0, 0, h], dst_ref=source_ref.at[index, rows(giver, h)],
                        send_sem=give_send.at[0, 0, h], recv_sem=give_recv.at[index, giver, h],
                        device_id=(blk, giver), device_id_type=MESH).wait_recv()

        if index == 0:
            pl.when(rep != 0)(arrive)
        else:
            arrive()


def gather_sources(features, tile_values, blocks, replicas):
    sections = tile_values.shape[1]
    rows, width = features.shape
    subs = 2 * largest_divisor(rows // replicas // 32, SUBS // 2)
    sub = rows // replicas // subs
    hops = blocks // 2
    vmem = pl.BlockSpec(memory_space=pltpu.VMEM)
    dma = pltpu.SemaphoreType.DMA
    return pl.pallas_call(
        functools.partial(gather_kernel, blocks, replicas, sections, subs),
        out_shape=(
            jax.ShapeDtypeStruct((sections, rows, width), features.dtype),
            jax.ShapeDtypeStruct(tile_values.shape, tile_values.dtype),
        ),
        in_specs=[vmem, pl.BlockSpec(memory_space=pl.ANY)],
        out_specs=(vmem, vmem),
        scratch_shapes=[
            pltpu.VMEM((2, hops, subs, sub, width), features.dtype),
            dma((2, hops, subs)), dma((2, hops, subs)), dma((2, hops, subs)),
            dma((sections, replicas, subs)), dma(()), dma(()),
        ],
        compiler_params=pltpu.CompilerParams(collective_id=1, has_side_effects=True, vmem_limit_bytes=2 * GRANT),
        cost_estimate=pl.CostEstimate(
            flops=0, bytes_accessed=96 * rows * width * features.dtype.itemsize, transcendentals=0
        ),
        name="gather_sources",
    )(features, tile_values)


def sections_kernel(find, group, place_ref, count_ref, source_ref, tiles_ref, acc_ref):
    step = pl.program_id(0)
    slots, tile = tiles_ref.shape[2], tiles_ref.shape[3]
    row_tiles = source_ref.shape[1] // tile
    section, chunk, active = find(step, count_ref)
    count = count_ref[0, section]
    base = chunk * slots

    @pl.when(step == 0)
    def _():
        acc_ref[...] = jnp.zeros_like(acc_ref)

    def body(g, carry):
        for u in range(group):
            k = g * group + u
            place = place_ref[0, section, base + k]
            column, target = lax.rem(place, row_tiles), lax.div(place, row_tiles)
            piece = source_ref[section, pl.ds(pl.multiple_of(column * tile, tile), tile), :]
            product = jnp.dot(tiles_ref[0, 0, k], piece, preferred_element_type=jnp.float32)
            rows = pl.ds(pl.multiple_of(target * tile, tile), tile)
            acc_ref[rows, :] += jnp.where(base + k < count, product, 0.0)
        return carry

    live = jnp.where(active, jnp.clip(count - base, 0, slots), 0)
    lax.fori_loop(0, (live + group - 1) // group, body, 0)


def section_sums(sources, tile_values, tile_place, tile_count):
    sections, slots, tile = tile_values.shape[1:4]
    rows, width = sources.shape[1:]
    block = largest_divisor(slots, BLOCK)
    group = largest_divisor(block, GROUP)

    def find(step, count_ref):
        section, chunk = jnp.int32(0), jnp.int32(0)
        start, active = jnp.int32(0), False
        for s in range(sections):
            steps = lax.div(count_ref[0, s] + block - 1, block)
            inside = step >= start
            section = jnp.where(inside, s, section)
            chunk = jnp.where(inside, jnp.minimum(step - start, steps - 1), chunk)
            start = start + steps
        return section, chunk, step < start

    def tiles_map(step, place_ref, count_ref):
        section, chunk, _ = find(step, count_ref)
        return (0, section, chunk, 0, 0)

    vmem = pl.BlockSpec(memory_space=pltpu.VMEM)
    return pl.pallas_call(
        functools.partial(sections_kernel, find, group),
        out_shape=jax.ShapeDtypeStruct((rows, width), jnp.float32),
        grid_spec=pltpu.PrefetchScalarGridSpec(
            num_scalar_prefetch=2, grid=(sections * slots // block,),
            in_specs=[vmem, pl.BlockSpec((1, 1, block, tile, tile), tiles_map)], out_specs=vmem
        ),
        compiler_params=pltpu.CompilerParams(vmem_limit_bytes=GRANT),
        name="section_sums",
    )(tile_place, tile_count, sources, tile_values)


def reduce_kernel(chips, chunks, part_ref, agg_ref, core_in, send_buf, recv_buf,
                  s1, r1, s2, r2, s3, r3, s4, r4):
    blk, rep = lax.axis_index("blk"), lax.axis_index("rep")
    core, chip = lax.rem(rep, 2), lax.div(rep, 2)
    rows = part_ref.shape[0]
    half = rows // 2
    size = half // chips // chunks
    other = chip * 2 + (1 - core)

    def peer(d):
        return lax.rem(chip + d, chips)

    def local(piece, ch):
        return pl.ds(pl.multiple_of((piece * chunks + ch) * size, size), size)

    def place(which, piece, ch):
        return pl.ds(pl.multiple_of(which * half + (piece * chunks + ch) * size, size), size)

    barrier = pltpu.get_barrier_semaphore()
    pl.semaphore_signal(barrier, inc=1, device_id=(blk, other), device_id_type=MESH)
    for d in range(1, chips):
        pl.semaphore_signal(barrier, inc=1, device_id=(blk, peer(d) * 2 + core), device_id_type=MESH)
    pl.semaphore_wait(barrier, chips)

    order = [(ch, d) for ch in range(chunks) for d in list(range(1, chips)) + [0]]
    stage1, stage2, stage3, stage4 = {}, {}, {}, {}
    for ch, d in order:
        copy = pltpu.make_async_remote_copy(
            src_ref=part_ref.at[place(1 - core, peer(d), ch)], dst_ref=core_in.at[local(peer(d), ch)],
            send_sem=s1.at[d, ch], recv_sem=r1.at[d, ch], device_id=(blk, other), device_id_type=MESH)
        copy.start()
        stage1[ch, d] = copy
    for ch, d in order:
        if d == 0:
            continue
        stage1[ch, d].wait_recv()
        total = part_ref[place(core, peer(d), ch), :] + core_in[local(peer(d), ch), :]
        send_buf[d - 1, ch] = total.astype(jnp.bfloat16)
        copy = pltpu.make_async_remote_copy(
            src_ref=send_buf.at[d - 1, ch], dst_ref=recv_buf.at[d - 1, ch],
            send_sem=s2.at[d, ch], recv_sem=r2.at[d, ch],
            device_id=(blk, peer(d) * 2 + core), device_id_type=MESH)
        copy.start()
        stage2[ch, d] = copy
    for ch in range(chunks):
        stage1[ch, 0].wait_recv()
        total = part_ref[place(core, chip, ch), :] + core_in[local(chip, ch), :]
        for d in range(1, chips):
            stage2[ch, d].wait_recv()
            total = total + recv_buf[d - 1, ch].astype(jnp.float32)
        mine = place(core, chip, ch)
        agg_ref[mine, :] = total.astype(jnp.bfloat16)
        for d in list(range(1, chips)) + [0]:
            target = other if d == 0 else peer(d) * 2 + core
            copy = pltpu.make_async_remote_copy(
                src_ref=agg_ref.at[mine], dst_ref=agg_ref.at[mine],
                send_sem=s3.at[d, ch], recv_sem=r3.at[d, ch],
                device_id=(blk, target), device_id_type=MESH)
            copy.start()
            stage3[ch, d] = copy
    for ch in range(chunks):
        for d in range(1, chips):
            stage3[ch, d].wait_recv()
            came = place(core, lax.rem(chip + chips - d, chips), ch)
            copy = pltpu.make_async_remote_copy(
                src_ref=agg_ref.at[came], dst_ref=agg_ref.at[came],
                send_sem=s4.at[d, ch], recv_sem=r4.at[d, ch],
                device_id=(blk, other), device_id_type=MESH)
            copy.start()
            stage4[ch, d] = copy
    for ch, d in order:
        stage1[ch, d].wait_send()
        stage3[ch, d].wait_send()
        if d == 0:
            stage3[ch, d].wait_recv()
        else:
            stage2[ch, d].wait_send()
            stage4[ch, d].wait()


def replica_sum(part, replicas):
    rows, width = part.shape
    chips = replicas // 2
    chunks = largest_divisor(rows // 2 // chips // 16, CHUNKS)
    size = rows // 2 // chips // chunks
    dma = pltpu.SemaphoreType.DMA((chips, chunks))
    vmem = pl.BlockSpec(memory_space=pltpu.VMEM)
    return pl.pallas_call(
        functools.partial(reduce_kernel, chips, chunks),
        out_shape=jax.ShapeDtypeStruct((rows, width), jnp.bfloat16),
        in_specs=[vmem],
        out_specs=vmem,
        scratch_shapes=[
            pltpu.VMEM((rows // 2, width), jnp.float32),
            pltpu.VMEM((chips - 1, chunks, size, width), jnp.bfloat16),
            pltpu.VMEM((chips - 1, chunks, size, width), jnp.bfloat16),
        ] + [dma] * 8,
        compiler_params=pltpu.CompilerParams(collective_id=0, has_side_effects=True, vmem_limit_bytes=GRANT),
        name="replica_sum",
    )(part)


def activate_kernel(agg_ref, weight_ref, bias_ref, out_ref):
    output = jnp.dot(agg_ref[...], weight_ref[...], preferred_element_type=jnp.float32) + bias_ref[...]
    out_ref[...] = jnp.maximum(output, 0.0).astype(out_ref.dtype)


def activate(aggregated, weight, bias):
    rows, width = aggregated.shape
    hidden = weight.shape[1]
    step = largest_divisor(rows, ROWS_STEP)
    return pl.pallas_call(
        activate_kernel,
        out_shape=jax.ShapeDtypeStruct((rows, hidden), jnp.bfloat16),
        grid=(rows // step,),
        in_specs=[
            pl.BlockSpec((step, width), lambda i: (i, 0)),
            pl.BlockSpec((width, hidden), lambda i: (0, 0)),
            pl.BlockSpec((1, hidden), lambda i: (0, 0)),
        ],
        out_specs=pl.BlockSpec((step, hidden), lambda i: (i, 0)),
        compiler_params=pltpu.CompilerParams(vmem_limit_bytes=GRANT),
        name="activate",
    )(aggregated, weight, bias[None, :])


def shards(blocks, replicas, features, weight, bias, tile_values, tile_place, tile_count):
    sources, held = gather_sources(features, tile_values, blocks, replicas)
    part = section_sums(sources, held, tile_place, tile_count)
    aggregated = replica_sum(part, replicas)
    return activate(aggregated, weight, bias)


def solution(mesh):
    in_specs = (
        P("blk", None),
        P(),
        P(),
        P("blk", "rep", None, None, None),
        P("blk", "rep", None),
        P("blk", "rep"),
    )
    body = functools.partial(shards, mesh.shape["blk"], mesh.shape["rep"])
    return jax.shard_map(body, mesh=mesh, in_specs=in_specs, out_specs=P("blk", None), check_vma=False)
```

profile of v0, /device:TPU:0, one launch (start us, length us, event | category | flops | bytes accessed | tf_op | source)
XLA Modules:
  0.0 61.6 jit_solution(7111980449838688645)
XLA Ops:
  0.0 0.0 copy-start
  0.0 1.2 %copy-done = bf16[4096,128]{1,0:T(8,128)(2,1)S(1)} copy-done((bf16[4096,128]{1,0:T(8,128)(2,1)S(1)}, bf16[4096,128]{1,0:T(8,128)(2,1)}, u32[]{:S(2)}) %copy-start) | copy-done | bytes 1048600
  1.2 0.0 copy-start.2
  1.2 0.0 copy-start.4
  1.2 37.0 %gather_sources.1 = (bf16[2,4096,128]{2,1,0:T(8,128)(2,1)S(1)}, bf16[1,2,160,128,128]{4,3,2,1,0:T(8,128)(2,1)S(1)}) custom-call(bf16[4096,128]{1,0:T(8,128)(2,1)S(1)} %copy-done, bf16[1,2,160,128,128]{4,3,2,1,0:T(8,128)(2,1)} %tiles_ref.1), custom_call_target="tpu_custom_call" | custom-call | bytes 100663296 | tf_op jit(solution)/shard_map/gather_sources/pallas_call | solution.py:136
  38.2 0.0 copy-done.2
  38.2 0.0 copy-done.4
  38.2 5.3 %section_sums.1.part_ref = f32[4096,128]{1,0:T(8,128)S(1)} custom-call(s32[1,2,160]{2,1,0:T(2,128)S(1)} %copy-done.2, s32[1,2]{1,0:T(1,128)S(1)} %copy-done.4, bf16[2,4096,128]{2,1,0:T(8,128)(2,1)S(1)} %get-tuple-element.7.source_ref, bf16[1,2,160,128,128]{4,3,2,1,0:T(8,128)(2,1)S(1)} %get-tuple-element.8.tiles_ref), custom_call_target="tpu_custom_call" | custom-call | tf_op jit(solution)/shard_map/section_sums/pallas_call | solution.py:206
  43.5 0.0 copy-start.1
  43.5 0.0 copy-start.3
  43.5 16.0 %replica_sum.1.agg_ref = bf16[4096,128]{1,0:T(8,128)(2,1)S(1)} custom-call(f32[4096,128]{1,0:T(8,128)S(1)} %section_sums.1.part_ref), custom_call_target="tpu_custom_call" | custom-call | tf_op jit(solution)/shard_map/replica_sum/pallas_call | solution.py:305
  59.5 0.0 copy-done.1
  59.5 0.0 copy-done.3
  59.5 2.0 %activate.1 = bf16[4096,256]{1,0:T(8,128)(2,1)} custom-call(bf16[4096,128]{1,0:T(8,128)(2,1)S(1)} %replica_sum.1.agg_ref, bf16[128,256]{1,0:T(8,128)(2,1)S(1)} %copy-done.1, f32[1,256]{1,0:T(1,128)S(1)} %bitcast.1), custom_call_target="tpu_custom_call" | custom-call | tf_op jit(solution)/shard_map/activate/pallas_call | solution.py:329
Async XLA Ops:
  0.0 1.2 %copy-start = (bf16[4096,128]{1,0:T(8,128)(2,1)S(1)}, bf16[4096,128]{1,0:T(8,128)(2,1)}, u32[]{:S(2)}) copy-start(bf16[4096,128]{1,0:T(8,128)(2,1)} %features_ref.1) | copy-start | bytes 3145732
  1.2 37.0 %copy-start.2 = (s32[1,2,160]{2,1,0:T(2,128)S(1)}, s32[1,2,160]{2,1,0:T(2,128)}, u32[]{:S(2)}) copy-start(s32[1,2,160]{2,1,0:T(2,128)} %place_ref.1) | copy-start | bytes 3844
  1.2 37.0 %copy-start.4 = (s32[1,2]{1,0:T(1,128)S(1)}, s32[1,2]{1,0:T(1,128)}, u32[]{:S(2)}) copy-start(s32[1,2]{1,0:T(1,128)} %count_ref.1) | copy-start | bytes 28
  43.5 16.0 %copy-start.1 = (bf16[128,256]{1,0:T(8,128)(2,1)S(1)}, bf16[128,256]{1,0:T(8,128)(2,1)}, u32[]{:S(2)}) copy-start(bf16[128,256]{1,0:T(8,128)(2,1)} %weight_ref.1) | copy-start | bytes 196612
  43.5 16.0 %copy-start.3 = (f32[256]{0:T(256)S(1)}, f32[256]{0:T(256)}, u32[]{:S(2)}) copy-start(f32[256]{0:T(256)} %param.8) | copy-start | bytes 3076
where the time goes:
time: 61.1 us; the launch traced here: 61.6 us
  Pallas kernels  60.2 us (99%)
  local copies, waits for them, and re-layouts  1.24 us (2%)
    pallas_call x1, Pallas kernels, gather_sources(): pl.pallas_call(functools.partial(gather_kernel, blocks, replicas, section...  37 us
    pallas_call x1, Pallas kernels, replica_sum(): pl.pallas_call(functools.partial(reduce_kernel, chips, chunks), out_shape...  16 us
    pallas_call x1, Pallas kernels, section_sums(): pl.pallas_call(functools.partial(sections_kernel, find, group), out_shape...  5.25 us
    pallas_call x1, Pallas kernels, activate(): pl.pallas_call(activate_kernel, out_shape=jax.ShapeDtypeStruct((rows, hid...  2.02 us
    unnamed x10, local copies, waits for them, and re-layouts  1.24 us

commit v1 on v0

--- a/solution.py
+++ b/solution.py
@@ -1,4 +1,5 @@
 import functools
+import heapq
 
 import jax
 import jax.numpy as jnp
@@ -11,7 +12,10 @@
 GROUP = 16
 BLOCK = 80
 CHUNKS = 4
-SUBS = 4
+PIECES = 16
+HOP = 4
+LEAD = 3
+PASSES = 1024
 ROWS_STEP = 4096
 GRANT = 16 * 1024 * 1024
 
@@ -20,133 +24,279 @@
     return max(d for d in range(1, most + 1) if number % d == 0)
 
 
-def gather_kernel(blocks, replicas, sections, subs, features_ref, tiles_ref, source_ref, held_ref, ring,
-                  ring_send, ring_recv, give_send, give_recv, own_sem, held_sem):
+def chip_grid(blocks, replicas):
+    columns = 2
+    planes = replicas // 2
+    chips = [(z, x, y) for z in range(blocks // columns) for x in range(columns) for y in range(planes)]
+    links = {}
+    for z, x, y in chips:
+        out = [(0, (z, columns - 1 - x, y)), (1, (z + 1, x, y)), (2, (z - 1, x, y))]
+        out += [(3, (z, x, 1 - y))] if planes == 2 else [(3, (z, x, y + 1)), (4, (z, x, y - 1))]
+        links[z, x, y] = [(way, chip) for way, chip in out if chip in set(chips)]
+    return columns, planes, chips, links
+
+
+def plan_trees(blocks, replicas, sections, pieces, hop, passes):
+    columns, planes, chips, links = chip_grid(blocks, replicas)
+    order = {chip: i for i, chip in enumerate(chips)}
+    core_of = {}
+    for b in range(blocks):
+        for r in range(replicas):
+            for i in range(sections):
+                core_of[(b // columns, b % columns, r // 2), (b - r * sections - i) % blocks] = r % 2
+    roots = {s: [(s // columns, s % columns, y) for y in range(planes)] for s in range(blocks)}
+    wants = {s: [c for c in chips if (c, s) in core_of and c not in roots[s]] for s in range(blocks)}
+    busy = {(chip, way): 0 for chip in chips for way, _ in links[chip]}
+    load = dict.fromkeys(busy, 0)
+    past = dict.fromkeys(busy, 0.0)
+    trees, best = {}, None
+    keys = [(s, p) for p in range(pieces) for s in range(blocks)]
+    turn, random = list(keys), 1
+
+    def grow(s, price):
+        ready = dict.fromkeys(roots[s], 0)
+        left, tree = set(wants[s]), []
+        while left:
+            cost, came, done = {}, {}, set()
+            heap = [(0.1 * t, t, order[c], c) for c, t in ready.items()]
+            heapq.heapify(heap)
+            while True:
+                c, t, _, chip = heapq.heappop(heap)
+                if chip in done:
+                    continue
+                done.add(chip)
+                if chip in left:
+                    break
+                for way, other in links[chip]:
+                    if other in ready or other in done:
+                        continue
+                    taken = busy[chip, way] >> t
+                    start = t + (~taken & (taken + 1)).bit_length() - 1
+                    total = c + 0.1 * (start + hop - t) + price[chip, way]
+                    if other not in cost or total < cost[other]:
+                        cost[other] = total
+                        came[other] = (chip, way, start)
+                        heapq.heappush(heap, (total, start + hop, order[other], other))
+            path = []
+            while chip not in ready:
+                path.append(came[chip] + (chip,))
+                chip = came[chip][0]
+            for chip, way, start, other in reversed(path):
+                ready[other] = start + hop
+                busy[chip, way] |= 1 << start
+                load[chip, way] += 1
+                tree.append((chip, way, start, other))
+                left.discard(other)
+        return tree
+
+    for _ in range(passes):
+        for key in turn:
+            for chip, way, start, _ in trees.get(key, ()):
+                busy[chip, way] &= ~(1 << start)
+                load[chip, way] -= 1
+            top = max(max(load.values()), 1)
+            trees[key] = grow(key[0], {k: past[k] + (load[k] / top) ** 4 for k in load})
+        last = {key: max(start for _, _, start, _ in tree) for key, tree in trees.items()}
+        span = max(last.values())
+        score = (span, sum(v >= span - 1 for v in last.values()), sum(load.values()))
+        if best is None or score < best[0]:
+            best = (score, {key: list(tree) for key, tree in trees.items()})
+        top = max(load.values())
+        for k in load:
+            past[k] = past[k] * 0.9 + (0.2 if load[k] >= top - pieces * 0.05 else 0.0)
+        ranks = []
+        for key in keys:
+            random = (random * 1103515245 + 12345) % (1 << 31)
+            ranks.append(((random >> 8) % 1000 / 125 - last[key], key))
+        turn = [key for _, key in sorted(ranks)]
+    return best[1], core_of
+
+
+def plan_gather(blocks, replicas, sections, pieces, hop, passes):
+    trees, core_of = plan_trees(blocks, replicas, sections, pieces, hop, passes)
+    columns, planes, chips, _ = chip_grid(blocks, replicas)
+    devices = blocks * replicas
+    actions = [[] for _ in range(devices)]
+    arrived = [set() for _ in range(devices)]
+
+    def core(chip, s, p):
+        return core_of.get((chip, s), p % 2) if chip[:2] != (s // columns, s % columns) else p % 2
+
+    def device(chip, c):
+        return (chip[0] * columns + chip[1]) * replicas + chip[2] * 2 + c
+
+    for (s, p), tree in sorted(trees.items()):
+        for chip, way, start, other in tree:
+            here, there = core(chip, s, p), core(other, s, p)
+            own = chip[:2] == (s // columns, s % columns)
+            actions[device(chip, here)].append((start - (LEAD if own else 0), not own, s * pieces + p, way, there))
+            arrived[device(other, there)].add(s * pieces + p)
+    plans = []
+    for d in range(devices):
+        slots, waited = [], set()
+        for _, relay, piece, way, there in sorted(actions[d]):
+            spot = None
+            for j in range(len(slots) - 1, -1, -1):
+                if slots[j][0] == piece:
+                    spot = j
+                    break
+                if way in slots[j][2]:
+                    break
+            if spot is None:
+                slots.append((piece, relay and piece not in waited, {}))
+                spot = len(slots) - 1
+                if relay:
+                    waited.add(piece)
+            slots[spot][2][way] = there
+        leaves = arrived[d] - waited
+        plans.append((slots, leaves))
+    return plans
+
+
+def gather_kernel(blocks, replicas, sections, pieces, plans, features_ref, tiles_ref, all_ref, held_ref,
+                  recv_sem, send_sem, own_sem, held_sem):
     blk, rep = lax.axis_index("blk"), lax.axis_index("rep")
-    share = features_ref.shape[0] // replicas
-    sub = share // subs
-    odd = lax.rem(blk, 2)
-    position = (1 - odd) * lax.div(blk, 2) + odd * (blocks - 1 - lax.div(blk, 2))
-
-    def block_at(offset):
-        p = lax.rem(position + blocks + offset, blocks)
-        back = lax.div(p, blocks // 2)
-        return (1 - back) * (2 * p) + back * (2 * (blocks - 1 - p) + 1)
-
-    def rows(who, h):
-        return pl.ds(pl.multiple_of(who * share + h * sub, sub), sub)
-
-    hops = blocks // 2
-    ways = (1, -1)
+    columns, planes, _, _ = chip_grid(blocks, replicas)
+    floors = blocks // columns
+    rows = features_ref.shape[0]
+    size = rows // pieces
+    z, x = lax.div(blk, columns), lax.rem(blk, columns)
+    y, me = lax.div(rep, 2), lax.rem(rep, 2)
+    is_blk = [blk == b for b in range(blocks)]
+    is_rep = [rep == r for r in range(replicas)]
+
+    def choose(options, tests):
+        value = jnp.int32(options[0])
+        for option, test in zip(options[1:], tests[1:]):
+            value = jnp.where(test, option, value)
+        return value
+
+    def pick(values):
+        if len(set(values)) == 1:
+            return jnp.int32(values[0])
+        picked = []
+        for b in range(blocks):
+            row = values[b * replicas:(b + 1) * replicas]
+            picked.append(row[0] if len(set(row)) == 1 else choose(row, is_rep))
+        return choose(picked, is_blk)
+
+    def target(way, c):
+        if way == 0:
+            return (z * columns + (columns - 1 - x), y * 2 + c)
+        if way in (1, 2):
+            return (blk + (columns if way == 1 else -columns), y * 2 + c)
+        if planes == 2:
+            return (blk, (1 - y) * 2 + c)
+        return (blk, (y + (1 if way == 3 else -1)) * 2 + c)
+
+    exists = {0: None, 1: z < floors - 1, 2: z > 0}
+    exists.update({3: None} if planes == 2 else {3: y < planes - 1, 4: y > 0})
+
+    own = pltpu.make_async_copy(features_ref, all_ref.at[blk], own_sem)
+    own.start()
     barrier = pltpu.get_barrier_semaphore()
-    for way in ways:
-        pl.semaphore_signal(barrier, inc=1, device_id=(block_at(way), rep), device_id_type=MESH)
-    for d in range(1, replicas):
-        pl.semaphore_signal(barrier, inc=1, device_id=(blk, lax.rem(rep + d, replicas)), device_id_type=MESH)
-    pl.semaphore_wait(barrier, replicas + 1)
-
-    def ring_copy(w, k, h):
-        source = features_ref.at[rows(rep, h)] if k == 0 else ring.at[w, k - 1, h]
+    count = jnp.int32(0)
+    for way, test in exists.items():
+        def greet(way=way):
+            for c in range(2):
+                pl.semaphore_signal(barrier, inc=1, device_id=target(way, c), device_id_type=MESH)
+        if test is None:
+            greet()
+            count = count + 2
+        else:
+            pl.when(test)(greet)
+            count = count + jnp.where(test, 2, 0)
+    pl.semaphore_wait(barrier, count)
+
+    def block(piece):
+        return all_ref.at[lax.div(piece, pieces), pl.ds(pl.multiple_of(lax.rem(piece, pieces) * size, size), size)]
+
+    def copy(piece, way, c, j):
         return pltpu.make_async_remote_copy(
-            src_ref=source, dst_ref=ring.at[w, k, h], send_sem=ring_send.at[w, k, h],
-            recv_sem=ring_recv.at[w, k, h], device_id=(block_at(ways[w]), rep), device_id_type=MESH)
-
-    def travels(w, k, h):
-        return k < hops - 1 or (k == hops - 1 and h * 2 // subs == w)
-
-    for h in range(subs):
-        for w in range(2):
-            if travels(w, 0, h):
-                ring_copy(w, 0, h).start()
+            src_ref=block(piece), dst_ref=block(piece), send_sem=send_sem.at[j, way],
+            recv_sem=recv_sem.at[piece], device_id=target(way, c), device_id_type=MESH)
+
+    steps = max(len(slots) for slots, _ in plans)
+    ways = len(exists)
+    table = []
+    for j in range(steps):
+        values, used, relays = [], set(), False
+        for slots, _ in plans:
+            if j >= len(slots):
+                values.append(0)
+                continue
+            piece, relay, sends = slots[j]
+            value = piece * 2 + int(relay)
+            for way in range(ways):
+                value = value * 4 + (2 + sends[way] if way in sends else 0)
+            used |= set(sends)
+            relays = relays or relay
+            values.append(value)
+        table.append((pick(values), used, relays))
+
+    def unpack(j):
+        value, used, relays = table[j]
+        head = lax.div(value, 4 ** ways)
+        piece = lax.div(head, 2)
+        sends = {}
+        for way in sorted(used):
+            field = lax.rem(lax.div(value, 4 ** (ways - 1 - way)), 4)
+            sends[way] = (field >= 2, lax.rem(field, 2))
+        return piece, lax.rem(head, 2) == 1, relays, sends
+
+    own.wait()
     held = pltpu.make_async_copy(tiles_ref, held_ref, held_sem)
-    held.start()
-    own = pltpu.make_async_copy(features_ref, source_ref.at[0], own_sem)
-
-    @pl.when(rep == 0)
-    def _():
-        own.start()
-
-    arrivals = [(k, h, w) for k in range(hops) for h in range(subs) for w in range(2) if travels(w, k, h)]
-
-    def give(k, h, w):
-        section = lax.rem(blk - block_at(-ways[w] * (k + 1)) + blocks, blocks)
-        target, index = lax.div(section, sections), lax.rem(section, sections)
-        place = source_ref.at[index, rows(rep, h)]
-        here = pltpu.make_async_copy(ring.at[w, k, h], place, give_send.at[w, k, h])
-        there = pltpu.make_async_remote_copy(
-            src_ref=ring.at[w, k, h], dst_ref=place, send_sem=give_send.at[w, k, h],
-            recv_sem=give_recv.at[index, rep, h], device_id=(blk, target), device_id_type=MESH)
-        return target, here, there
-
-    for k, h, w in arrivals:
-        ring_copy(w, k, h).wait_recv()
-        if travels(w, k + 1, h):
-            ring_copy(w, k + 1, h).start()
-        target, here, there = give(k, h, w)
-
-        @pl.when(target == rep)
-        def _():
-            here.start()
-
-        @pl.when(target != rep)
-        def _():
-            there.start()
-
-    for k, h, w in arrivals:
-        ring_copy(w, k, h).wait_send()
-        target, here, there = give(k, h, w)
-
-        @pl.when(target == rep)
-        def _():
-            here.wait()
-
-        @pl.when(target != rep)
-        def _():
-            there.wait_send()
-
-    @pl.when(rep == 0)
-    def _():
-        own.wait()
-
+    for j in range(steps):
+        piece, relay, relays, sends = unpack(j)
+        if relays:
+            pl.when(relay)(lambda piece=piece, j=j: copy(piece, 0, 0, j).wait_recv())
+        for way, (test, c) in sends.items():
+            pl.when(test)(lambda piece=piece, way=way, c=c, j=j: copy(piece, way, c, j).start())
+        if j == 3:
+            held.start()
+
+    def drain(j):
+        piece, _, _, sends = unpack(j)
+        for way, (test, c) in sends.items():
+            pl.when(test)(lambda piece=piece, way=way, c=c, j=j: copy(piece, way, c, j).wait_send())
+
+    for j in range(steps * 3 // 4):
+        drain(j)
     held.wait()
-    for index in range(sections):
-        def arrive(index=index):
-            for d in range(1, replicas):
-                giver = lax.rem(rep + d, replicas)
-                for h in range(subs):
-                    pltpu.make_async_remote_copy(
-                        src_ref=ring.at[0, 0, h], dst_ref=source_ref.at[index, rows(giver, h)],
-                        send_sem=give_send.at[0, 0, h], recv_sem=give_recv.at[index, giver, h],
-                        device_id=(blk, giver), device_id_type=MESH).wait_recv()
-
-        if index == 0:
-            pl.when(rep != 0)(arrive)
-        else:
-            arrive()
+    for i in range(sections):
+        source = lax.rem(blk - rep * sections - i + blocks, blocks)
+        values = []
+        for d, (_, leaves) in enumerate(plans):
+            s = (d // replicas - d % replicas * sections - i) % blocks
+            values.append(sum(1 << p for p in range(pieces) if s * pieces + p in leaves))
+        mask = pick(values)
+        for p in range(pieces):
+            if any(v >> p & 1 for v in values):
+                test = lax.rem(lax.div(mask, 1 << p), 2) == 1
+                pl.when(test)(lambda p=p, source=source: copy(source * pieces + p, 0, 0, 0).wait_recv())
+    for j in range(steps * 3 // 4, steps):
+        drain(j)
 
 
 def gather_sources(features, tile_values, blocks, replicas):
     sections = tile_values.shape[1]
     rows, width = features.shape
-    subs = 2 * largest_divisor(rows // replicas // 32, SUBS // 2)
-    sub = rows // replicas // subs
-    hops = blocks // 2
+    pieces = largest_divisor(rows // 16, PIECES)
+    plans = plan_gather(blocks, replicas, sections, pieces, HOP, max(2, PASSES // (blocks * replicas)))
+    steps = max(len(slots) for slots, _ in plans)
     vmem = pl.BlockSpec(memory_space=pltpu.VMEM)
+    hbm = pl.BlockSpec(memory_space=pl.ANY)
     dma = pltpu.SemaphoreType.DMA
     return pl.pallas_call(
-        functools.partial(gather_kernel, blocks, replicas, sections, subs),
+        functools.partial(gather_kernel, blocks, replicas, sections, pieces, plans),
         out_shape=(
-            jax.ShapeDtypeStruct((sections, rows, width), features.dtype),
+            jax.ShapeDtypeStruct((blocks, rows, width), features.dtype),
             jax.ShapeDtypeStruct(tile_values.shape, tile_values.dtype),
         ),
-        in_specs=[vmem, pl.BlockSpec(memory_space=pl.ANY)],
+        in_specs=[hbm, hbm],
         out_specs=(vmem, vmem),
-        scratch_shapes=[
-            pltpu.VMEM((2, hops, subs, sub, width), features.dtype),
-            dma((2, hops, subs)), dma((2, hops, subs)), dma((2, hops, subs)),
-            dma((sections, replicas, subs)), dma(()), dma(()),
-        ],
-        compiler_params=pltpu.CompilerParams(collective_id=1, has_side_effects=True, vmem_limit_bytes=2 * GRANT),
+        scratch_shapes=[dma((blocks * pieces,)), dma((steps, 5)), dma(()), dma(())],
+        compiler_params=pltpu.CompilerParams(collective_id=1, has_side_effects=True, vmem_limit_bytes=3 * GRANT),
         cost_estimate=pl.CostEstimate(
             flops=0, bytes_accessed=96 * rows * width * features.dtype.itemsize, transcendentals=0
         ),
@@ -154,11 +304,14 @@
     )(features, tile_values)
 
 
-def sections_kernel(find, group, place_ref, count_ref, source_ref, tiles_ref, acc_ref):
+def sections_kernel(find, group, sections, place_ref, count_ref, source_ref, tiles_ref, acc_ref):
     step = pl.program_id(0)
     slots, tile = tiles_ref.shape[2], tiles_ref.shape[3]
     row_tiles = source_ref.shape[1] // tile
+    blocks = source_ref.shape[0]
     section, chunk, active = find(step, count_ref)
+    blk, rep = lax.axis_index("blk"), lax.axis_index("rep")
+    source = lax.rem(blk - rep * sections - section + blocks, blocks)
     count = count_ref[0, section]
     base = chunk * slots
 
@@ -171,7 +324,7 @@
             k = g * group + u
             place = place_ref[0, section, base + k]
             column, target = lax.rem(place, row_tiles), lax.div(place, row_tiles)
-            piece = source_ref[section, pl.ds(pl.multiple_of(column * tile, tile), tile), :]
+            piece = source_ref[source, pl.ds(pl.multiple_of(column * tile, tile), tile), :]
             product = jnp.dot(tiles_ref[0, 0, k], piece, preferred_element_type=jnp.float32)
             rows = pl.ds(pl.multiple_of(target * tile, tile), tile)
             acc_ref[rows, :] += jnp.where(base + k < count, product, 0.0)
@@ -204,7 +357,7 @@
 
     vmem = pl.BlockSpec(memory_space=pltpu.VMEM)
     return pl.pallas_call(
-        functools.partial(sections_kernel, find, group),
+        functools.partial(sections_kernel, find, group, sections),
         out_shape=jax.ShapeDtypeStruct((rows, width), jnp.float32),
         grid_spec=pltpu.PrefetchScalarGridSpec(
             num_scalar_prefetch=2, grid=(sections * slots // block,),

time: 61.1 us -> 73.3 us (1.20)
  local copies, waits for them, and re-layouts: 1.24 us -> 8.61 us
  Pallas kernels: 60.2 us -> 64.6 us
    unnamed x10 -> x14, local copies, waits for them, and re-layouts: 1.24 us -> 8.61 us
    pallas_call x1, Pallas kernels: 37 us -> 41.5 us  [gather_sources(): pl.pallas_call(functools.partial(gather_kernel, blocks, replicas, section...]
    pallas_call x1, Pallas kernels: 5.25 us -> 2.15 us  [section_sums(): pl.pallas_call(functools.partial(sections_kernel, find, group, sections),...]
    pallas_call x1, Pallas kernels: 16 us -> 18.9 us  [replica_sum(): pl.pallas_call(functools.partial(reduce_kernel, chips, chunks), out_shape...]
where the time goes in v1:
time: 73.3 us
  Pallas kernels  64.6 us (88%)
  local copies, waits for them, and re-layouts  8.61 us (12%)
    pallas_call x1, Pallas kernels, gather_sources(): pl.pallas_call(functools.partial(gather_kernel, blocks, replicas, section...  41.5 us
    pallas_call x1, Pallas kernels, replica_sum(): pl.pallas_call(functools.partial(reduce_kernel, chips, chunks), out_shape...  18.9 us
    unnamed x14, local copies, waits for them, and re-layouts  8.61 us
    pallas_call x1, Pallas kernels, section_sums(): pl.pallas_call(functools.partial(sections_kernel, find, group, sections),...  2.15 us
    pallas_call x1, Pallas kernels, activate(): pl.pallas_call(activate_kernel, out_shape=jax.ShapeDtypeStruct((rows, hid...  2.01 us

profile of v1, /device:TPU:0, one launch (start us, length us, event | category | flops | bytes accessed | tf_op | source)
XLA Modules:
  0.0 73.3 jit_solution(4134070015094100006)
XLA Ops:
  0.0 0.0 copy-start.6
  0.0 0.0 copy-start.2
  0.0 1.2 %copy-done.2 = bf16[4096,128]{1,0:T(8,128)(2,1)S(1)} copy-done((bf16[4096,128]{1,0:T(8,128)(2,1)S(1)}, bf16[4096,128]{1,0:T(8,128)(2,1)}, u32[]{:S(2)}) %copy-start.2) | copy-done | bytes 1048600
  1.2 0.0 copy-start.4
  1.2 41.5 %gather_sources.1 = (bf16[8,4096,128]{2,1,0:T(8,128)(2,1)}, bf16[1,2,160,128,128]{4,3,2,1,0:T(8,128)(2,1)}) custom-call(bf16[4096,128]{1,0:T(8,128)(2,1)S(1)} %copy-done.2, bf16[1,2,160,128,128]{4,3,2,1,0:T(8,128)(2,1)} %tiles_ref.1), custom_call_target="tpu_custom_call" | custom-call | bytes 100663296 | tf_op jit(solution)/shard_map/gather_sources/pallas_call | solution.py:290
  42.8 0.0 copy-done.6
  42.8 0.0 copy-done.4
  42.8 0.0 copy-start
  42.8 4.0 %copy-done = bf16[1,2,160,128,128]{4,3,2,1,0:T(8,128)(2,1)S(1)} copy-done((bf16[1,2,160,128,128]{4,3,2,1,0:T(8,128)(2,1)S(1)}, bf16[1,2,160,128,128]{4,3,2,1,0:T(8,128)(2,1)}, u32[]{:S(2)}) %copy-start) | copy-done | bytes 10485784
  46.8 0.0 copy-start.1
  46.8 3.4 %copy-done.1 = bf16[8,4096,128]{2,1,0:T(8,128)(2,1)S(1)} copy-done((bf16[8,4096,128]{2,1,0:T(8,128)(2,1)S(1)}, bf16[8,4096,128]{2,1,0:T(8,128)(2,1)}, u32[]{:S(2)}) %copy-start.1) | copy-done | bytes 8388632
  50.2 0.0 copy-start.3
  50.2 0.0 copy-start.5
  50.2 2.2 %section_sums.1.part_ref = f32[4096,128]{1,0:T(8,128)S(1)} custom-call(s32[1,2,160]{2,1,0:T(2,128)S(1)} %copy-done.4, s32[1,2]{1,0:T(1,128)S(1)} %copy-done.6, bf16[8,4096,128]{2,1,0:T(8,128)(2,1)S(1)} %copy-done.1, bf16[1,2,160,128,128]{4,3,2,1,0:T(8,128)(2,1)S(1)} %copy-done), custom_call_target="tpu_custom_call" | custom-call | tf_op jit(solution)/shard_map/section_sums/pallas_call | solution.py:359
  52.3 18.9 %replica_sum.1.agg_ref = bf16[4096,128]{1,0:T(8,128)(2,1)S(1)} custom-call(f32[4096,128]{1,0:T(8,128)S(1)} %section_sums.1.part_ref), custom_call_target="tpu_custom_call" | custom-call | tf_op jit(solution)/shard_map/replica_sum/pallas_call | solution.py:458
  71.2 0.0 copy-done.3
  71.3 0.0 copy-done.5
  71.3 2.0 %activate.1 = bf16[4096,256]{1,0:T(8,128)(2,1)} custom-call(bf16[4096,128]{1,0:T(8,128)(2,1)S(1)} %replica_sum.1.agg_ref, bf16[128,256]{1,0:T(8,128)(2,1)S(1)} %copy-done.3, f32[1,256]{1,0:T(1,128)S(1)} %bitcast.1), custom_call_target="tpu_custom_call" | custom-call | tf_op jit(solution)/shard_map/activate/pallas_call | solution.py:482
Async XLA Ops:
  0.0 42.8 %copy-start.6 = (s32[1,2]{1,0:T(1,128)S(1)}, s32[1,2]{1,0:T(1,128)}, u32[]{:S(2)}) copy-start(s32[1,2]{1,0:T(1,128)} %count_ref.1) | copy-start | bytes 28
  0.0 1.2 %copy-start.2 = (bf16[4096,128]{1,0:T(8,128)(2,1)S(1)}, bf16[4096,128]{1,0:T(8,128)(2,1)}, u32[]{:S(2)}) copy-start(bf16[4096,128]{1,0:T(8,128)(2,1)} %features_ref.1) | copy-start | bytes 3145732
  1.2 41.6 %copy-start.4 = (s32[1,2,160]{2,1,0:T(2,128)S(1)}, s32[1,2,160]{2,1,0:T(2,128)}, u32[]{:S(2)}) copy-start(s32[1,2,160]{2,1,0:T(2,128)} %place_ref.1) | copy-start | bytes 3844
  42.8 4.0 %copy-start = (bf16[1,2,160,128,128]{4,3,2,1,0:T(8,128)(2,1)S(1)}, bf16[1,2,160,128,128]{4,3,2,1,0:T(8,128)(2,1)}, u32[]{:S(2)}) copy-start(bf16[1,2,160,128,128]{4,3,2,1,0:T(8,128)(2,1)} %get-tuple-element.8.tiles_ref) | copy-start | bytes 31457284
  46.8 3.4 %copy-start.1 = (bf16[8,4096,128]{2,1,0:T(8,128)(2,1)S(1)}, bf16[8,4096,128]{2,1,0:T(8,128)(2,1)}, u32[]{:S(2)}) copy-start(bf16[8,4096,128]{2,1,0:T(8,128)(2,1)} %get-tuple-element.7.source_ref) | copy-start | bytes 25165828
  50.2 21.1 %copy-start.3 = (bf16[128,256]{1,0:T(8,128)(2,1)S(1)}, bf16[128,256]{1,0:T(8,128)(2,1)}, u32[]{:S(2)}) copy-start(bf16[128,256]{1,0:T(8,128)(2,1)} %weight_ref.1) | copy-start | bytes 196612
  50.2 21.1 %copy-start.5 = (f32[256]{0:T(256)S(1)}, f32[256]{0:T(256)}, u32[]{:S(2)}) copy-start(f32[256]{0:T(256)} %param.8) | copy-start | bytes 3076

commit v2 on v1

--- a/solution.py
+++ b/solution.py
@@ -285,7 +285,7 @@
     plans = plan_gather(blocks, replicas, sections, pieces, HOP, max(2, PASSES // (blocks * replicas)))
     steps = max(len(slots) for slots, _ in plans)
     vmem = pl.BlockSpec(memory_space=pltpu.VMEM)
-    hbm = pl.BlockSpec(memory_space=pl.ANY)
+    hbm = pl.BlockSpec(memory_space=pltpu.HBM)
     dma = pltpu.SemaphoreType.DMA
     return pl.pallas_call(
         functools.partial(gather_kernel, blocks, replicas, sections, pieces, plans),
@@ -296,7 +296,7 @@
         in_specs=[hbm, hbm],
         out_specs=(vmem, vmem),
         scratch_shapes=[dma((blocks * pieces,)), dma((steps, 5)), dma(()), dma(())],
-        compiler_params=pltpu.CompilerParams(collective_id=1, has_side_effects=True, vmem_limit_bytes=3 * GRANT),
+        compiler_params=pltpu.CompilerParams(collective_id=1, has_side_effects=True, vmem_limit_bytes=2 * GRANT),
         cost_estimate=pl.CostEstimate(
             flops=0, bytes_accessed=96 * rows * width * features.dtype.itemsize, transcendentals=0
         ),

time: 73.3 us -> 59.9 us (0.82)
  local copies, waits for them, and re-layouts: 8.61 us -> 1.26 us
  Pallas kernels: 64.6 us -> 58.4 us
    unnamed x14 -> x10, local copies, waits for them, and re-layouts: 8.61 us -> 1.26 us
    pallas_call x1, Pallas kernels: 41.5 us -> 35.1 us  [gather_sources(): pl.pallas_call(functools.partial(gather_kernel, blocks, replicas, section...]
    pallas_call x1, Pallas kernels: 2.15 us -> 4.66 us  [section_sums(): pl.pallas_call(functools.partial(sections_kernel, find, group, sections),...]
    pallas_call x1, Pallas kernels: 18.9 us -> 16.6 us  [replica_sum(): pl.pallas_call(functools.partial(reduce_kernel, chips, chunks), out_shape...]
where the time goes in v2:
time: 59.9 us; the launch traced here: 59.7 us
  Pallas kernels  58.4 us (97%)
  local copies, waits for them, and re-layouts  1.26 us (2%)
    pallas_call x1, Pallas kernels, gather_sources(): pl.pallas_call(functools.partial(gather_kernel, blocks, replicas, section...  35.1 us
    pallas_call x1, Pallas kernels, replica_sum(): pl.pallas_call(functools.partial(reduce_kernel, chips, chunks), out_shape...  16.6 us
    pallas_call x1, Pallas kernels, section_sums(): pl.pallas_call(functools.partial(sections_kernel, find, group, sections),...  4.66 us
    pallas_call x1, Pallas kernels, activate(): pl.pallas_call(activate_kernel, out_shape=jax.ShapeDtypeStruct((rows, hid...  2.01 us
    unnamed x10, local copies, waits for them, and re-layouts  1.26 us

profile of v2, /device:TPU:0, one launch (start us, length us, event | category | flops | bytes accessed | tf_op | source)
XLA Modules:
  0.0 59.7 jit_solution(16670756225553947956)
XLA Ops:
  0.0 0.0 copy-start.4
  0.0 0.0 copy-start
  0.0 1.2 %copy-done = bf16[4096,128]{1,0:T(8,128)(2,1)S(1)} copy-done((bf16[4096,128]{1,0:T(8,128)(2,1)S(1)}, bf16[4096,128]{1,0:T(8,128)(2,1)}, u32[]{:S(2)}) %copy-start) | copy-done | bytes 1048600
  1.2 0.0 copy-start.2
  1.2 35.1 %gather_sources.1 = (bf16[8,4096,128]{2,1,0:T(8,128)(2,1)S(1)}, bf16[1,2,160,128,128]{4,3,2,1,0:T(8,128)(2,1)S(1)}) custom-call(bf16[4096,128]{1,0:T(8,128)(2,1)S(1)} %copy-done, bf16[1,2,160,128,128]{4,3,2,1,0:T(8,128)(2,1)} %tiles_ref.1), custom_call_target="tpu_custom_call" | custom-call | bytes 100663296 | tf_op jit(solution)/shard_map/gather_sources/pallas_call | solution.py:290
  36.3 0.0 copy-done.4
  36.3 0.0 copy-done.2
  36.3 0.0 copy-start.1
  36.4 0.0 copy-start.3
  36.4 4.7 %section_sums.1.part_ref = f32[4096,128]{1,0:T(8,128)S(1)} custom-call(s32[1,2,160]{2,1,0:T(2,128)S(1)} %copy-done.2, s32[1,2]{1,0:T(1,128)S(1)} %copy-done.4, bf16[8,4096,128]{2,1,0:T(8,128)(2,1)S(1)} %get-tuple-element.7.source_ref, bf16[1,2,160,128,128]{4,3,2,1,0:T(8,128)(2,1)S(1)} %get-tuple-element.8.tiles_ref), custom_call_target="tpu_custom_call" | custom-call | tf_op jit(solution)/shard_map/section_sums/pallas_call | solution.py:359
  41.0 16.6 %replica_sum.1.agg_ref = bf16[4096,128]{1,0:T(8,128)(2,1)S(1)} custom-call(f32[4096,128]{1,0:T(8,128)S(1)} %section_sums.1.part_ref), custom_call_target="tpu_custom_call" | custom-call | tf_op jit(solution)/shard_map/replica_sum/pallas_call | solution.py:458
  57.7 0.0 copy-done.1
  57.7 0.0 copy-done.3
  57.7 2.0 %activate.1 = bf16[4096,256]{1,0:T(8,128)(2,1)} custom-call(bf16[4096,128]{1,0:T(8,128)(2,1)S(1)} %replica_sum.1.agg_ref, bf16[128,256]{1,0:T(8,128)(2,1)S(1)} %copy-done.1, f32[1,256]{1,0:T(1,128)S(1)} %bitcast.1), custom_call_target="tpu_custom_call" | custom-call | tf_op jit(solution)/shard_map/activate/pallas_call | solution.py:482
Async XLA Ops:
  0.0 36.3 %copy-start.4 = (s32[1,2]{1,0:T(1,128)S(1)}, s32[1,2]{1,0:T(1,128)}, u32[]{:S(2)}) copy-start(s32[1,2]{1,0:T(1,128)} %count_ref.1) | copy-start | bytes 28
  0.0 1.2 %copy-start = (bf16[4096,128]{1,0:T(8,128)(2,1)S(1)}, bf16[4096,128]{1,0:T(8,128)(2,1)}, u32[]{:S(2)}) copy-start(bf16[4096,128]{1,0:T(8,128)(2,1)} %features_ref.1) | copy-start | bytes 3145732
  1.2 35.1 %copy-start.2 = (s32[1,2,160]{2,1,0:T(2,128)S(1)}, s32[1,2,160]{2,1,0:T(2,128)}, u32[]{:S(2)}) copy-start(s32[1,2,160]{2,1,0:T(2,128)} %place_ref.1) | copy-start | bytes 3844
  36.3 21.3 %copy-start.1 = (bf16[128,256]{1,0:T(8,128)(2,1)S(1)}, bf16[128,256]{1,0:T(8,128)(2,1)}, u32[]{:S(2)}) copy-start(bf16[128,256]{1,0:T(8,128)(2,1)} %weight_ref.1) | copy-start | bytes 196612
  36.4 21.3 %copy-start.3 = (f32[256]{0:T(256)S(1)}, f32[256]{0:T(256)}, u32[]{:S(2)}) copy-start(f32[256]{0:T(256)} %param.8) | copy-start | bytes 3076

commit v3 on v2

--- a/solution.py
+++ b/solution.py
@@ -16,7 +16,8 @@
 HOP = 4
 LEAD = 3
 PASSES = 1024
-ROWS_STEP = 4096
+ROWS_STEP = 1024
+SWAPS = 8
 GRANT = 16 * 1024 * 1024
 
 
@@ -301,7 +302,7 @@
             flops=0, bytes_accessed=96 * rows * width * features.dtype.itemsize, transcendentals=0
         ),
         name="gather_sources",
-    )(features, tile_values)
+    )(pltpu.with_memory_space_constraint(features, pltpu.HBM), tile_values)
 
 
 def sections_kernel(find, group, sections, place_ref, count_ref, source_ref, tiles_ref, acc_ref):
@@ -366,6 +367,70 @@
         compiler_params=pltpu.CompilerParams(vmem_limit_bytes=GRANT),
         name="section_sums",
     )(tile_place, tile_count, sources, tile_values)
+
+
+def swap_kernel(chunks, part_ref, agg_ref, core_in, send_buf, recv_buf, s1, r1, s2, r2, s3, r3):
+    blk, rep = lax.axis_index("blk"), lax.axis_index("rep")
+    core, chip = lax.rem(rep, 2), lax.div(rep, 2)
+    half = part_ref.shape[0] // 2
+    size = half // chunks
+    other, across = chip * 2 + (1 - core), (1 - chip) * 2 + core
+
+    def place(which, ch):
+        return pl.ds(pl.multiple_of(which * half + ch * size, size), size)
+
+    barrier = pltpu.get_barrier_semaphore()
+    for target in (other, across):
+        pl.semaphore_signal(barrier, inc=1, device_id=(blk, target), device_id_type=MESH)
+    pl.semaphore_wait(barrier, 2)
+
+    stage1, stage2, stage3 = [], [], []
+    for ch in range(chunks):
+        stage1.append(pltpu.make_async_remote_copy(
+            src_ref=part_ref.at[place(1 - core, ch)], dst_ref=core_in.at[ch],
+            send_sem=s1.at[ch], recv_sem=r1.at[ch], device_id=(blk, other), device_id_type=MESH))
+        stage1[ch].start()
+    for ch in range(chunks):
+        stage1[ch].wait_recv()
+        send_buf[ch] = (part_ref[place(core, ch), :] + core_in[ch]).astype(send_buf.dtype)
+        stage2.append(pltpu.make_async_remote_copy(
+            src_ref=send_buf.at[ch], dst_ref=recv_buf.at[ch],
+            send_sem=s2.at[ch], recv_sem=r2.at[ch], device_id=(blk, across), device_id_type=MESH))
+        stage2[ch].start()
+    for ch in range(chunks):
+        stage2[ch].wait_recv()
+        mine = place(core, ch)
+        total = send_buf[ch].astype(jnp.float32) + recv_buf[ch].astype(jnp.float32)
+        agg_ref[mine, :] = total.astype(agg_ref.dtype)
+        stage3.append(pltpu.make_async_remote_copy(
+            src_ref=agg_ref.at[mine], dst_ref=agg_ref.at[mine],
+            send_sem=s3.at[ch], recv_sem=r3.at[ch], device_id=(blk, other), device_id_type=MESH))
+        stage3[ch].start()
+    for ch in range(chunks):
+        stage1[ch].wait_send()
+        stage2[ch].wait_send()
+        stage3[ch].wait()
+
+
+def pair_sum(part):
+    rows, width = part.shape
+    chunks = largest_divisor(rows // 2 // 16, SWAPS)
+    size = rows // 2 // chunks
+    dma = pltpu.SemaphoreType.DMA((chunks,))
+    vmem = pl.BlockSpec(memory_space=pltpu.VMEM)
+    return pl.pallas_call(
+        functools.partial(swap_kernel, chunks),
+        out_shape=jax.ShapeDtypeStruct((rows, width), jnp.bfloat16),
+        in_specs=[vmem],
+        out_specs=vmem,
+        scratch_shapes=[
+            pltpu.VMEM((chunks, size, width), jnp.float32),
+            pltpu.VMEM((chunks, size, width), jnp.bfloat16),
+            pltpu.VMEM((chunks, size, width), jnp.bfloat16),
+        ] + [dma] * 6,
+        compiler_params=pltpu.CompilerParams(collective_id=0, has_side_effects=True, vmem_limit_bytes=GRANT),
+        name="replica_sum",
+    )(part)
 
 
 def reduce_kernel(chips, chunks, part_ref, agg_ref, core_in, send_buf, recv_buf,
@@ -497,7 +562,7 @@
 def shards(blocks, replicas, features, weight, bias, tile_values, tile_place, tile_count):
     sources, held = gather_sources(features, tile_values, blocks, replicas)
     part = section_sums(sources, held, tile_place, tile_count)
-    aggregated = replica_sum(part, replicas)
+    aggregated = pair_sum(part) if replicas == 4 else replica_sum(part, replicas)
     return activate(aggregated, weight, bias)
 
 

time: 59.9 us -> 59.4 us (level); the launches traced: 59.7 us -> 58.5 us
  local copies, waits for them, and re-layouts: 1.26 us -> 0.02 us
    pallas_call x1, Pallas kernels: 4.66 us -> 1.85 us  [section_sums(): pl.pallas_call(functools.partial(sections_kernel, find, group, sections),...]
    pallas_call x1, Pallas kernels: 16.6 us -> 19.1 us  [pair_sum(): pl.pallas_call(functools.partial(swap_kernel, chunks), out_shape=jax.Shap...]
    unnamed x10 -> x8, local copies, waits for them, and re-layouts: 1.26 us -> 0.02 us
where the time goes in v3:
time: 59.4 us; the launch traced here: 58.5 us
  Pallas kernels  58.4 us (98%)
    pallas_call x1, Pallas kernels, gather_sources(): pl.pallas_call(functools.partial(gather_kernel, blocks, replicas, section...  35 us
    pallas_call x1, Pallas kernels, pair_sum(): pl.pallas_call(functools.partial(swap_kernel, chunks), out_shape=jax.Shap...  19.1 us
    pallas_call x1, Pallas kernels, activate(): pl.pallas_call(activate_kernel, out_shape=jax.ShapeDtypeStruct((rows, hid...  2.48 us
    pallas_call x1, Pallas kernels, section_sums(): pl.pallas_call(functools.partial(sections_kernel, find, group, sections),...  1.85 us

profile of v3, /device:TPU:0, one launch (start us, length us, event | category | flops | bytes accessed | tf_op | source)
XLA Modules:
  0.0 58.5 jit_solution(14709972675121436679)
XLA Ops:
  0.0 0.0 copy-start.3
  0.0 0.0 copy-start.1
  0.0 35.0 %gather_sources.1 = (bf16[8,4096,128]{2,1,0:T(8,128)(2,1)S(1)}, bf16[1,2,160,128,128]{4,3,2,1,0:T(8,128)(2,1)S(1)}) custom-call(bf16[4096,128]{1,0:T(8,128)(2,1)} %features_ref.1, bf16[1,2,160,128,128]{4,3,2,1,0:T(8,128)(2,1)} %tiles_ref.1), custom_call_target="tpu_custom_call" | custom-call | bytes 100663296 | tf_op jit(solution)/shard_map/gather_sources/pallas_call | solution.py:291
  35.0 0.0 copy-done.3
  35.0 0.0 copy-done.1
  35.0 0.0 copy-start
  35.0 0.0 copy-start.2
  35.1 1.8 %section_sums.1.part_ref = f32[4096,128]{1,0:T(8,128)S(1)} custom-call(s32[1,2,160]{2,1,0:T(2,128)S(1)} %copy-done.1, s32[1,2]{1,0:T(1,128)S(1)} %copy-done.3, bf16[8,4096,128]{2,1,0:T(8,128)(2,1)S(1)} %get-tuple-element.7.source_ref, bf16[1,2,160,128,128]{4,3,2,1,0:T(8,128)(2,1)S(1)} %get-tuple-element.8.tiles_ref), custom_call_target="tpu_custom_call" | custom-call | tf_op jit(solution)/shard_map/section_sums/pallas_call | solution.py:360
  36.9 19.1 %replica_sum.1.agg_ref = bf16[4096,128]{1,0:T(8,128)(2,1)S(1)} custom-call(f32[4096,128]{1,0:T(8,128)S(1)} %section_sums.1.part_ref), custom_call_target="tpu_custom_call" | custom-call | tf_op jit(solution)/shard_map/replica_sum/pallas_call | solution.py:421
  56.0 0.0 copy-done
  56.0 0.0 copy-done.2
  56.0 2.5 %activate.1 = bf16[4096,256]{1,0:T(8,128)(2,1)} custom-call(bf16[4096,128]{1,0:T(8,128)(2,1)S(1)} %replica_sum.1.agg_ref, bf16[128,256]{1,0:T(8,128)(2,1)S(1)} %copy-done, f32[1,256]{1,0:T(1,128)S(1)} %bitcast.1), custom_call_target="tpu_custom_call" | custom-call | tf_op jit(solution)/shard_map/activate/pallas_call | solution.py:547
Async XLA Ops:
  0.0 35.0 %copy-start.3 = (s32[1,2]{1,0:T(1,128)S(1)}, s32[1,2]{1,0:T(1,128)}, u32[]{:S(2)}) copy-start(s32[1,2]{1,0:T(1,128)} %count_ref.1) | copy-start | bytes 28
  0.0 35.0 %copy-start.1 = (s32[1,2,160]{2,1,0:T(2,128)S(1)}, s32[1,2,160]{2,1,0:T(2,128)}, u32[]{:S(2)}) copy-start(s32[1,2,160]{2,1,0:T(2,128)} %place_ref.1) | copy-start | bytes 3844
  35.0 21.0 %copy-start = (bf16[128,256]{1,0:T(8,128)(2,1)S(1)}, bf16[128,256]{1,0:T(8,128)(2,1)}, u32[]{:S(2)}) copy-start(bf16[128,256]{1,0:T(8,128)(2,1)} %weight_ref.1) | copy-start | bytes 196612
  35.0 21.0 %copy-start.2 = (f32[256]{0:T(256)S(1)}, f32[256]{0:T(256)}, u32[]{:S(2)}) copy-start(f32[256]{0:T(256)} %param.8) | copy-start | bytes 3076
